TPU v7x, 256 devices: a whole 4x4x8 slice. The times are simulated.
256 devices in a mesh: pix: 64 (over x, z, core), band: 4 (over y).
Axes of the slice: x: 4, y: 4, z: 8, core: 2. Of those that a mesh axis runs over, the one named last changes fastest.
Arguments:
- spectra: bfloat16 [224, 262144], P('band', 'pix'), may hold values from -0.1 to 4
- endmembers: bfloat16 [224, 512], P('band'), may hold values from 0.05 to 1
- gram_inverse: float32 [512, 512], replicated, may hold values from -1 to 1, as said below
- abundances: float32 [512, 262144], P(None, ('pix', 'band')), may hold values from 0 to 512, as said below
- duals: float32 [512, 262144], P(None, ('pix', 'band')), may hold values from -4 to 4
Outputs:
- abundances_out: float32 [512, 262144], P(None, ('pix', 'band'))
- duals_out: float32 [512, 262144], P(None, ('pix', 'band'))
- residual_rms: float32 [2, 2], replicated
Inputs may be any that keep to these rules, and one draw needn't show every extreme that they name: `abundances`: each column is nonnegative and sums to 512. `gram_inverse`: penalty times the float32 inverse of endmembers^T endmembers / 512^2 + penalty I, with penalty = 224 / (2 * 512^2) and the endmembers as stored.
All inputs are finite; a program needn't handle non-finite values.
Results may differ from a plain program's by a relative error of at most 0.0004.
Values may be sent and summed in bfloat16 or wider, within the bound.
A program may use at most 64 MiB of HBM per device.

v0:
```python
import jax
import jax.numpy as jnp
from jax import lax
from jax.sharding import Mesh
from jax.sharding import PartitionSpec as P

B = 224
K = 512
ITERS = 2
BISECT = 6
PIX = ("pix_0", "pix_1", "pix_2")
PIX_BAND = ("pix_0", "pix_1", "pix_2", "band")


def one_axis_at_a_time(shard, axes):
    for axis in axes:
        shard = lax.psum(shard, axis)
    return shard


def project(shifted):
    simplex_sum = float(K)
    high_end = jnp.max(shifted, axis=0)
    low_end = (jnp.sum(shifted, axis=0) - simplex_sum) / simplex_sum

    def mass_at(level):
        return jnp.sum(jnp.maximum(shifted - level[None, :], 0.0), axis=0)

    mass_low = mass_at(low_end)
    mass_high = jnp.zeros_like(high_end)

    def bisect_once(unused, state):
        low_now, high_now, low_mass, high_mass = state
        middle = 0.5 * (low_now + high_now)
        total_mass = mass_at(middle)
        too_high = total_mass > simplex_sum
        return (
            jnp.where(too_high, middle, low_now),
            jnp.where(too_high, high_now, middle),
            jnp.where(too_high, total_mass, low_mass),
            jnp.where(too_high, high_mass, total_mass),
        )

    low_end, high_end, mass_low, mass_high = lax.fori_loop(
        0, BISECT, bisect_once, (low_end, high_end, mass_low, mass_high)
    )
    level = low_end + (mass_low - simplex_sum) * (high_end - low_end) / (mass_low - mass_high)
    return jnp.maximum(shifted - level[None, :], 0.0)


def contract_bands(signatures, columns):
    return lax.dot_general(
        signatures, columns, (((0,), (0,)), ((), ())), preferred_element_type=jnp.float32
    )


def body(spectra, endmembers, gram_inverse, abundances, duals):
    penalty = B / (2.0 * K * K)
    exchanged = lax.all_to_all(spectra, "band", split_axis=1, concat_axis=0, tiled=True)
    all_rows = lax.all_gather(endmembers, "band", axis=0, tiled=True)
    fit_term = contract_bands(all_rows, exchanged)
    fit_term = fit_term / K
    pixel_count = abundances.shape[1] * lax.axis_size(PIX) * lax.axis_size("band")
    current = abundances
    scaled_dual = duals
    primal_list = []
    change_list = []
    for sweep in range(ITERS):
        primal = jnp.dot(
            gram_inverse,
            fit_term / penalty + current - scaled_dual,
            precision=lax.Precision.HIGHEST,
        )
        updated = project(primal + scaled_dual)
        scaled_dual = scaled_dual + primal - updated
        primal_sum = jnp.sum((primal - updated) ** 2)
        change_sum = jnp.sum((updated - current) ** 2)
        primal_list.append(primal_sum)
        change_list.append(change_sum)
        current = updated
    totals = jnp.stack([jnp.stack(primal_list), jnp.stack(change_list)])
    totals = one_axis_at_a_time(totals, PIX_BAND)
    residual_rms = jnp.sqrt(totals / pixel_count)
    return (current, scaled_dual, residual_rms)


def solution(mesh):
    finer = Mesh(
        mesh.devices.reshape(4, 8, 2, mesh.shape["band"]), ("pix_0", "pix_1", "pix_2", "band")
    )
    return jax.shard_map(
        body,
        mesh=finer,
        in_specs=(P("band", PIX), P("band", None), P(), P(None, PIX_BAND), P(None, PIX_BAND)),
        out_specs=(P(None, PIX_BAND), P(None, PIX_BAND), P()),
        check_vma=False,
    )
```

profile of v0, /device:TPU:1, one launch (start us, length us, event | category | flops | bytes accessed | tf_op | source)
XLA Modules:
  0.0 109.2 jit_solution(441457199507730125)
XLA Ops:
  0.6 0.0 copy-start
  0.6 1.9 %copy.12 = bf16[7,4,8,1024]{3,2,0,1:T(8,128)(2,1)} copy(bf16[7,4,8,1024]{3,2,1,0:T(8,128)(2,1)} %bitcast.36) | data formatting | bytes 917504 | tf_op jit(solution)/shard_map/all_to_all | solution.py:59
  2.5 5.0 %all-to-all-start = ((bf16[56,4,1024]{2,0,1:T(8,128)(2,1)}), bf16[56,4,1024]{2,0,1:T(8,128)(2,1)S(1)}, u32[]{:S(2)}, u32[]{:S(2)}) async-start(bf16[56,4,1024]{2,0,1:T(8,128)(2,1)} %bitcast.34), calls=%async_computation | async-start | bytes 917504 | tf_op jit(solution)/shard_map/all_to_all | solution.py:59
  7.6 12.5 %all_gather.3 = bf16[224,512]{1,0:T(8,128)(2,1)S(1)} all-gather(bf16[56,512]{1,0:T(8,128)(2,1)} %param.10), channel_id=1, replica_groups=mesh['pix_0'=4,'pix_1'=8,'pix_2'=2,'band'=4] {'band'}, dimensions={0}, use_global_device_ids=true | all-gather | bytes 286720 | tf_op jit(solution)/shard_map/all_gather | solution.py:60
  20.0 0.0 all-to-all-done
  20.0 0.5 fusion.29
  20.5 0.0 copy-done
  20.5 0.0 copy-start.2
  20.5 8.7 %fusion.28 = (f32[1024]{0:T(1024)S(1)}, f32[512,1024]{1,0:T(8,128)S(1)}, f32[1024,512]{0,1:T(8,128)}) fusion(f32[512,1024]{1,0:T(8,128)} %param.13, f32[512,512]{1,0:T(8,128)S(1)} %copy-done, f32[512,1024]{1,0:T(8,128)} %param.12, f32[512,1024]{1,0:T(8,128)S(1)} %fusion.29), kind=kOutput, calls=%fused_computation.54 | convolution fusion | flops 3223845888 | bytes 11538432 | tf_op jit(solution)/shard_map/dot_general | solution.py:69
  29.2 0.0 copy-done.2
  29.2 0.3 maximum_reduce_fusion.3
  29.5 1.9 %while.34 = (s32[]{:T(128)}, f32[1024]{0:T(1024)S(1)}, f32[1024]{0:T(1024)S(1)}, f32[1024]{0:T(1024)S(1)}, f32[1024]{0:T(1024)S(1)}, /*index=5*/f32[512,1024]{1,0:T(8,128)S(1)}, s32[]{:T(128)}, s32[]{:T(128)}) while((s32[]{:T(128)}, f32[1024]{0:T(1024)S(1)}, f32[1024]{0:T(1024)S(1)}, f32[1024]{0:T(1024)S(1)}, f32[1024]{0:T(1024)S(1)}, ...), condition=%wide.region_5.6_spmd.clone, body=%wide.region_3.5_spmd.clone.sunk | while | flops 1582083 | bytes 2154591 | solution.py:44
  29.6 0.3 maximum_reduce_fusion.6
  29.9 0.3 maximum_reduce_fusion.6
  30.2 0.3 maximum_reduce_fusion.6
  30.5 0.3 maximum_reduce_fusion.6
  30.8 0.3 maximum_reduce_fusion.6
  31.2 0.3 maximum_reduce_fusion.6
  31.5 7.0 %fusion.27 = (f32[1024]{0:T(1024)S(1)}, f32[512,1024]{1,0:T(8,128)S(1)}, f32[1024,512]{0,1:T(8,128)}) fusion(f32[512,1024]{1,0:T(8,128)S(1)} %get-tuple-element.310, f32[1024]{0:T(1024)S(1)} %divide_add_fusion.1, f32[512,512]{1,0:T(8,128)S(1)} %copy-done, f32[512,1024]{1,0:T(8,128)} %copy-done.2), kind=kOutput, calls=%fused_computation.53 | convolution fusion | flops 3226991616 | bytes 9445376 | tf_op jit(solution)/shard_map/dot_general | solution.py:69
  38.5 0.0 copy-start.1
  38.5 0.3 maximum_reduce_fusion.2
  38.8 1.0 copy-done.1
  39.8 11.3 %while.35 = (s32[]{:T(128)}, f32[1024]{0:T(1024)S(1)}, f32[1024]{0:T(1024)S(1)}, f32[1024]{0:T(1024)S(1)}, f32[1024]{0:T(1024)S(1)}, /*index=5*/f32[512,1024]{1,0:T(8,128)}, s32[]{:T(128)}, s32[]{:T(128)}) while((s32[]{:T(128)}, f32[1024]{0:T(1024)S(1)}, f32[1024]{0:T(1024)S(1)}, f32[1024]{0:T(1024)S(1)}, f32[1024]{0:T(1024)S(1)}, ...), condition=%wide.region_11.12_spmd.clone, body=%wide.region_9.0_spmd.clone.sunk | while | flops 1582083 | bytes 2154591 | solution.py:44
  39.8 1.8 %maximum_reduce_fusion.7 = f32[1024]{0:T(1024)S(1)} fusion(f32[512,1024]{1,0:T(8,128)} %get-tuple-element.307, f32[1024]{0:T(1024)S(1)} %add_multiply_fusion.7), kind=kLoop, calls=%fused_computation.7.clone.1 | loop fusion | flops 1571840 | bytes 2105344 | tf_op jit(solution)/shard_map/while/body/eval_jaxpr/reduce_sum | solution.py:27
  41.7 1.8 %maximum_reduce_fusion.7 = f32[1024]{0:T(1024)S(1)} fusion(f32[512,1024]{1,0:T(8,128)} %get-tuple-element.307, f32[1024]{0:T(1024)S(1)} %add_multiply_fusion.7), kind=kLoop, calls=%fused_computation.7.clone.1 | loop fusion | flops 1571840 | bytes 2105344 | tf_op jit(solution)/shard_map/while/body/eval_jaxpr/reduce_sum | solution.py:27
  43.6 1.8 %maximum_reduce_fusion.7 = f32[1024]{0:T(1024)S(1)} fusion(f32[512,1024]{1,0:T(8,128)} %get-tuple-element.307, f32[1024]{0:T(1024)S(1)} %add_multiply_fusion.7), kind=kLoop, calls=%fused_computation.7.clone.1 | loop fusion | flops 1571840 | bytes 2105344 | tf_op jit(solution)/shard_map/while/body/eval_jaxpr/reduce_sum | solution.py:27
  45.5 1.8 %maximum_reduce_fusion.7 = f32[1024]{0:T(1024)S(1)} fusion(f32[512,1024]{1,0:T(8,128)} %get-tuple-element.307, f32[1024]{0:T(1024)S(1)} %add_multiply_fusion.7), kind=kLoop, calls=%fused_computation.7.clone.1 | loop fusion | flops 1571840 | bytes 2105344 | tf_op jit(solution)/shard_map/while/body/eval_jaxpr/reduce_sum | solution.py:27
  47.3 1.8 %maximum_reduce_fusion.7 = f32[1024]{0:T(1024)S(1)} fusion(f32[512,1024]{1,0:T(8,128)} %get-tuple-element.307, f32[1024]{0:T(1024)S(1)} %add_multiply_fusion.7), kind=kLoop, calls=%fused_computation.7.clone.1 | loop fusion | flops 1571840 | bytes 2105344 | tf_op jit(solution)/shard_map/while/body/eval_jaxpr/reduce_sum | solution.py:27
  49.2 1.8 %maximum_reduce_fusion.7 = f32[1024]{0:T(1024)S(1)} fusion(f32[512,1024]{1,0:T(8,128)} %get-tuple-element.307, f32[1024]{0:T(1024)S(1)} %add_multiply_fusion.7), kind=kLoop, calls=%fused_computation.7.clone.1 | loop fusion | flops 1571840 | bytes 2105344 | tf_op jit(solution)/shard_map/while/body/eval_jaxpr/reduce_sum | solution.py:27
  51.1 7.0 %fusion.9 = (f32[]{:T(128)}, f32[]{:T(128)}, f32[]{:T(128)}, f32[]{:T(128)}, f32[512,1024]{1,0:T(8,128)}) fusion(f32[1024,512]{0,1:T(8,128)} %get-tuple-element.168, f32[512,1024]{1,0:T(8,128)S(1)} %get-tuple-element.310, f32[1024]{0:T(1024)S(1)} %divide_add_fusion.1, f32[512,1024]{1,0:T(8,128)} %param.12, f32[1024,512]{0,1:T(8,128)} %get-tuple-element.169, ...), kind=kLoop, calls=%fused_computation.21 | loop fusion | flops 8388604 | bytes 12591120 | tf_op jit(solution)/shard_map/reduce_sum | solution.py:76
  58.1 2.6 %maximum_bitcast_fusion = (f32[1,2]{1,0:T(1,128)S(1)}, f32[1,2]{1,0:T(1,128)S(1)}) fusion(f32[1]{0:T(128)} %bitcast.5, f32[1]{0:T(128)} %bitcast.4, f32[1]{0:T(128)} %bitcast.8, f32[1]{0:T(128)} %bitcast.7), kind=kLoop, calls=%fused_computation.48 | loop fusion | flops 4 | bytes 32 | tf_op jit(solution)/shard_map/stack | solution.py:81
  60.7 8.0 %psum.28 = f32[2,2]{1,0:T(2,128)S(1)} all-reduce(f32[2,2]{1,0:T(2,128)S(1)} %pad_maximum_fusion), channel_id=1, replica_groups=mesh['pix_0'=4,'pix_1'=8,'pix_2'=2,'band'=4] {'pix_0'}, use_global_device_ids=true, to_apply=%region_16.17 | all-reduce | flops 4 | bytes 32 | tf_op jit(solution)/shard_map/psum | solution.py:17
  68.8 16.2 %psum.29 = f32[2,2]{1,0:T(2,128)S(1)} all-reduce(f32[2,2]{1,0:T(2,128)S(1)} %psum.28), channel_id=1, replica_groups=mesh['pix_0'=4,'pix_1'=8,'pix_2'=2,'band'=4] {'pix_1'}, use_global_device_ids=true, to_apply=%region_17.18 | all-reduce | flops 4 | bytes 32 | tf_op jit(solution)/shard_map/psum | solution.py:17
  85.0 12.4 %psum.30 = f32[2,2]{1,0:T(2,128)S(1)} all-reduce(f32[2,2]{1,0:T(2,128)S(1)} %psum.29), channel_id=1, replica_groups=mesh['pix_0'=4,'pix_1'=8,'pix_2'=2,'band'=4] {'pix_2'}, use_global_device_ids=true, to_apply=%region_18.19 | all-reduce | flops 4 | bytes 32 | tf_op jit(solution)/shard_map/psum | solution.py:17
  97.4 7.1 %psum.31 = f32[2,2]{1,0:T(2,128)S(1)} all-reduce(f32[2,2]{1,0:T(2,128)S(1)} %psum.30), channel_id=1, replica_groups=mesh['pix_0'=4,'pix_1'=8,'pix_2'=2,'band'=4] {'band'}, use_global_device_ids=true, to_apply=%region_19.20 | all-reduce | flops 4 | bytes 32 | tf_op jit(solution)/shard_map/psum | solution.py:17
  104.5 0.6 multiply_sqrt_fusion
  105.1 4.1 %sub.115 = f32[512,1024]{1,0:T(8,128)} subtract(f32[512,1024]{1,0:T(8,128)} %get-tuple-element.311, f32[512,1024]{1,0:T(8,128)} %get-tuple-element.155) | non-fusion elementwise | flops 524288 | bytes 6291456 | tf_op jit(solution)/shard_map/sub | solution.py:75
  (31 shorter events, 0.2 us)
Async XLA Ops:
  0.6 19.9 %copy-start = (f32[512,512]{1,0:T(8,128)S(1)}, f32[512,512]{1,0:T(8,128)}, u32[]{:S(2)}) copy-start(f32[512,512]{1,0:T(8,128)} %param.11) | copy-start | bytes 3145732
  2.5 17.5 %all-to-all-start = ((bf16[56,4,1024]{2,0,1:T(8,128)(2,1)}), bf16[56,4,1024]{2,0,1:T(8,128)(2,1)S(1)}, u32[]{:S(2)}, u32[]{:S(2)}) async-start(bf16[56,4,1024]{2,0,1:T(8,128)(2,1)} %bitcast.34), calls=%async_computation | async-start | bytes 917504 | tf_op jit(solution)/shard_map/all_to_all | solution.py:59
  20.5 8.7 %copy-start.2 = (f32[512,1024]{1,0:T(8,128)}, f32[512,1024]{1,0:T(8,128)S(1)}, u32[]{:S(2)}) copy-start(f32[512,1024]{1,0:T(8,128)S(1)} %fusion.29) | copy-start | bytes 6291460
  38.5 1.4 %copy-start.1 = (f32[512,1024]{1,0:T(8,128)}, f32[512,1024]{1,0:T(8,128)S(1)}, u32[]{:S(2)}) copy-start(f32[512,1024]{1,0:T(8,128)S(1)} %get-tuple-element.291) | copy-start | bytes 6291460
where the time goes:
time: 110 us; the launch traced here: 109 us
  blocking collectives  56.2 us (51%)
  other arithmetic  27.9 us (25%)
  matrix products  16.1 us (15%)
  starting transfers between devices  5 us (5%)
  local copies, waits for them, and re-layouts  2.93 us (3%)
    psum x4, blocking collectives, one_axis_at_a_time(): shard = lax.psum(shard, axis)  43.7 us
    dot_general x2, matrix products, body(): jnp.dot(gram_inverse, fit_term / penalty + current - scaled_dual, precisi...  15.7 us
    reduce_sum x14, other arithmetic, mass_at(): return jnp.sum(jnp.maximum(shifted - level[None, :], 0.0), axis=0)  13.3 us
    all_gather x1, blocking collectives, body(): all_rows = lax.all_gather(endmembers, 'band', axis=0, tiled=True)  12.5 us
    reduce_sum x1, other arithmetic, body(): primal_sum = jnp.sum((primal - updated) ** 2)  7.01 us
    all_to_all x1, starting transfers between devices, body(): lax.all_to_all(spectra, 'band', split_axis=1, concat_axis=0, tiled=True)  5 us
    sub x1, other arithmetic, body(): scaled_dual = scaled_dual + primal - updated  4.1 us
    another operation x2, other arithmetic, body(): totals = jnp.stack([jnp.stack(primal_list), jnp.stack(change_list)])  2.64 us
  transfers between devices with their start and end apart: 1, of which 0 were waited for; matrix products, arithmetic and copies ran while one was open for 0% of the time, Pallas kernels for 0%

commit v1 on v0

--- a/solution.py
+++ b/solution.py
@@ -10,6 +10,18 @@
 BISECT = 6
 PIX = ("pix_0", "pix_1", "pix_2")
 PIX_BAND = ("pix_0", "pix_1", "pix_2", "band")
+
+
+def sent_to_each(x, axis, split, join):
+    ways, here = (lax.axis_size(axis), lax.axis_index(axis))
+    width = x.shape[split] // ways
+    turned = jnp.roll(x, -here * width, axis=split)
+    got = [lax.slice_in_dim(turned, 0, width, axis=split)]
+    for far in range(1, ways):
+        sent = lax.slice_in_dim(turned, far * width, (far + 1) * width, axis=split)
+        got.append(lax.ppermute(sent, axis, [(d, (d + far) % ways) for d in range(ways)]))
+    line = jnp.concatenate(got[::-1], axis=join)
+    return jnp.roll(line, (here + 1) * got[0].shape[join], axis=join)
 
 
 def one_axis_at_a_time(shard, axes):
@@ -56,7 +68,7 @@
 
 def body(spectra, endmembers, gram_inverse, abundances, duals):
     penalty = B / (2.0 * K * K)
-    exchanged = lax.all_to_all(spectra, "band", split_axis=1, concat_axis=0, tiled=True)
+    exchanged = sent_to_each(spectra, "band", 1, 0)
     all_rows = lax.all_gather(endmembers, "band", axis=0, tiled=True)
     fit_term = contract_bands(all_rows, exchanged)
     fit_term = fit_term / K

time: 110 us -> 112 us (1.018)
  local copies, waits for them, and re-layouts: 2.93 us -> 17.7 us
  other arithmetic: 27.9 us -> 18.7 us
  blocking collectives: 56.2 us -> 54.2 us
  matrix products: 16.1 us -> 14.6 us
    unnamed x6 -> x25, local copies, waits for them, and re-layouts: 1.02 us -> 16 us
    reduce_sum x14, other arithmetic: 13.3 us -> 7.65 us  [mass_at(): return jnp.sum(jnp.maximum(shifted - level[None, :], 0.0), axis=0)]
    ppermute x0 -> x3, starting transfers between devices: none -> 5.22 us  [sent_to_each(): lax.ppermute(sent, axis, [(d, (d + far) % ways) for d in range(ways)])]
    all_to_all x1 -> x0, starting transfers between devices: 5 us -> none  [body(): lax.all_to_all(spectra, 'band', split_axis=1, concat_axis=0, tiled=True)]
    sub x1 -> x0, other arithmetic: 4.1 us -> none  [body(): scaled_dual = scaled_dual + primal - updated]
    all_gather x1, blocking collectives: 12.5 us -> 10.2 us  [body(): all_rows = lax.all_gather(endmembers, 'band', axis=0, tiled=True)]
    all_to_all x1 -> x0, local copies, waits for them, and re-layouts: 1.9 us -> none  [body(): lax.all_to_all(spectra, 'band', split_axis=1, concat_axis=0, tiled=True)]
    dot_general x2, matrix products: 15.7 us -> 14.1 us  [body(): jnp.dot(gram_inverse, fit_term / penalty + current - scaled_dual, precisi...]
  transfers between devices with their start and end apart: 1 -> 3, of which waited for: 0 -> 0; matrix products, arithmetic and copies ran while one was open for 0% -> 5% of each run, Pallas kernels for 0% -> 0%
where the time goes in v1:
time: 112 us
  blocking collectives  54.2 us (48%)
  other arithmetic  18.7 us (17%)
  local copies, waits for them, and re-layouts  17.7 us (16%)
  matrix products  14.6 us (13%)
  starting transfers between devices  5.22 us (5%)
    psum x4, blocking collectives, one_axis_at_a_time(): shard = lax.psum(shard, axis)  44 us
    unnamed x25, local copies, waits for them, and re-layouts  16 us
    dot_general x2, matrix products, body(): jnp.dot(gram_inverse, fit_term / penalty + current - scaled_dual, precisi...  14.1 us
    all_gather x1, blocking collectives, body(): all_rows = lax.all_gather(endmembers, 'band', axis=0, tiled=True)  10.2 us
    reduce_sum x14, other arithmetic, mass_at(): return jnp.sum(jnp.maximum(shifted - level[None, :], 0.0), axis=0)  7.65 us
    reduce_sum x1, other arithmetic, body(): primal_sum = jnp.sum((primal - updated) ** 2)  6.42 us
    ppermute x3, starting transfers between devices, sent_to_each(): lax.ppermute(sent, axis, [(d, (d + far) % ways) for d in range(ways)])  5.22 us
    another operation x2, other arithmetic, body(): totals = jnp.stack([jnp.stack(primal_list), jnp.stack(change_list)])  2.57 us
  transfers between devices with their start and end apart: 3, of which 0 were waited for; matrix products, arithmetic and copies ran while one was open for 5% of the time, Pallas kernels for 0%

profile of v1, /device:TPU:1, one launch (start us, length us, event | category | flops | bytes accessed | tf_op | source)
XLA Modules:
  0.0 111.6 jit_solution(9933235363385726759)
XLA Ops:
  0.6 0.0 copy-start
  0.7 1.3 %fusion.24 = bf16[56,4096]{1,0:T(8,128)(2,1)S(1)} fusion(s32[]{:T(128)S(6)} %select_n.49, bf16[56,4096]{1,0:T(8,128)(2,1)} %param.9), kind=kLoop, calls=%fused_computation.43 | loop fusion | flops 917504 | bytes 917508 | tf_op jit(solution)/shard_map/jit(_roll_dynamic)/concatenate | solution.py:18
  2.0 0.0 copy-start.4
  2.0 0.8 copy-done.4
  2.7 0.7 fusion.34
  3.5 3.6 %collective-permute-start = (bf16[56,1024]{1,0:T(8,128)(2,1)}, bf16[56,1024]{1,0:T(8,128)(2,1)S(1)}, u32[]{:S(2)}, u32[]{:S(2)}) collective-permute-start(bf16[56,1024]{1,0:T(8,128)(2,1)} %get-tuple-element.186), channel_id=1, source_target_pairs={{0,3},{1,0},{2,1},{3,2},{4,7},{5,4},{6,5},{7,6},{8,11},{9,8},{10,9... | collective-permute-start | bytes 344072 | tf_op jit(solution)/shard_map/ppermute | solution.py:22
  7.1 0.0 collective-permute-start.2
  7.1 1.7 %collective-permute-start.1 = (bf16[56,1024]{1,0:T(8,128)(2,1)}, bf16[56,1024]{1,0:T(8,128)(2,1)S(1)}, u32[]{:S(2)}, u32[]{:S(2)}) collective-permute-start(bf16[56,1024]{1,0:T(8,128)(2,1)} %get-tuple-element.185), channel_id=1, source_target_pairs={{0,2},{1,3},{2,0},{3,1},{4,6},{5,7},{6,4},{7,5},{8,10},{9,11},{10,... | collective-permute-start | bytes 344072 | tf_op jit(solution)/shard_map/ppermute | solution.py:22
  8.7 1.9 %copy.8 = f32[512,1024]{0,1:T(8,128)S(1)} copy(f32[512,1024]{1,0:T(8,128)} %param.12) | data formatting | bytes 4194304 | tf_op args[3]
  10.6 0.0 copy-start.1
  10.7 0.0 copy-start.5
  10.7 3.7 %copy.9 = f32[512,1024]{0,1:T(8,128)} copy(f32[512,1024]{1,0:T(8,128)} %param.13) | data formatting | bytes 4194304 | tf_op args[4]
  14.3 0.0 copy-done.5
  14.3 10.2 %all_gather.3 = bf16[224,512]{1,0:T(8,128)(2,1)S(1)} all-gather(bf16[56,512]{1,0:T(8,128)(2,1)S(1)} %copy-done.5), channel_id=1, replica_groups=mesh['pix_0'=4,'pix_1'=8,'pix_2'=2,'band'=4] {'band'}, dimensions={0}, use_global_device_ids=true | all-gather | bytes 286720 | tf_op jit(solution)/shard_map/all_gather | solution.py:72
  24.6 0.0 collective-permute-done
  24.6 0.0 collective-permute-done.1
  24.6 0.0 copy-start.3
  24.6 0.0 collective-permute-done.2
  24.6 1.1 slice_dynamic-update-slice_fusion
  25.7 0.9 slice_dynamic-update-slice_fusion.1
  26.6 0.5 fusion.25
  27.1 0.0 copy-done.1
  27.1 0.0 copy-done
  27.1 0.0 copy-done.3
  27.2 0.0 copy-start.2
  27.2 5.3 %fusion.33 = (f32[1024]{0:T(1024)S(1)}, f32[512,1024]{0,1:T(8,128)}, f32[1024,512]{1,0:T(8,128)}) fusion(f32[512,1024]{0,1:T(8,128)S(1)} %copy-done.3, f32[512,512]{1,0:T(8,128)S(1)} %copy-done, f32[512,1024]{0,1:T(8,128)S(1)} %copy.8, f32[1024,512]{1,0:T(8,128)S(1)} %fusion.25), kind=kOutput, calls=%fused_computation.68 | convolution fusion | flops 3223845888 | bytes 11538432 | tf_op jit(solution)/shard_map/dot_general | solution.py:81
  32.4 0.0 copy-done.2
  32.4 1.9 %copy.12 = f32[512,1024]{1,0:T(8,128)S(1)} copy(f32[512,1024]{0,1:T(8,128)} %get-tuple-element.173) | data formatting | bytes 4194304
  34.4 2.2 %maximum_reduce_fusion.3 = (f32[1024]{0:T(1024)S(1)}, f32[1024]{0:T(1024)S(1)}) fusion(f32[512,1024]{0,1:T(8,128)} %get-tuple-element.173, f32[1024]{0:T(1024)S(1)} %add_multiply_fusion.3), kind=kLoop, calls=%fused_computation.34 | loop fusion | flops 2095104 | bytes 2109440 | tf_op jit(solution)/shard_map/reduce_sum | solution.py:39
  36.5 1.9 %while.34 = (s32[]{:T(128)}, f32[1024]{0:T(1024)S(1)}, f32[1024]{0:T(1024)S(1)}, f32[1024]{0:T(1024)S(1)}, f32[1024]{0:T(1024)S(1)}, /*index=5*/f32[512,1024]{1,0:T(8,128)S(1)}, s32[]{:T(128)}, s32[]{:T(128)}) while((s32[]{:T(128)}, f32[1024]{0:T(1024)S(1)}, f32[1024]{0:T(1024)S(1)}, f32[1024]{0:T(1024)S(1)}, f32[1024]{0:T(1024)S(1)}, ...), condition=%wide.region_5.6_spmd.clone, body=%wide.region_3.5_spmd.clone.sunk | while | flops 1582083 | bytes 2154591 | solution.py:56
  36.6 0.3 maximum_reduce_fusion.6
  36.9 0.3 maximum_reduce_fusion.6
  37.2 0.3 maximum_reduce_fusion.6
  37.5 0.3 maximum_reduce_fusion.6
  37.8 0.3 maximum_reduce_fusion.6
  38.2 0.3 maximum_reduce_fusion.6
  38.5 8.9 %fusion.32 = (f32[1024]{0:T(1024)S(1)}, f32[512,1024]{0,1:T(8,128)}, f32[1024,512]{1,0:T(8,128)}) fusion(f32[512,1024]{0,1:T(8,128)} %get-tuple-element.173, f32[1024]{0:T(1024)S(1)} %divide_add_fusion.1, f32[512,512]{1,0:T(8,128)S(1)} %copy-done, f32[1024,512]{1,0:T(8,128)} %copy-done.2), kind=kOutput, calls=%fused_computation.67 | convolution fusion | flops 3226991616 | bytes 9445376 | tf_op jit(solution)/shard_map/dot_general | solution.py:81
  47.3 1.9 %copy.14 = f32[512,1024]{1,0:T(8,128)S(1)} copy(f32[512,1024]{0,1:T(8,128)} %get-tuple-element.171) | data formatting | bytes 4194304
  49.3 2.2 %maximum_reduce_fusion.2 = (f32[1024]{0:T(1024)S(1)}, f32[1024]{0:T(1024)S(1)}) fusion(f32[512,1024]{0,1:T(8,128)} %get-tuple-element.171, f32[1024]{0:T(1024)S(1)} %add_multiply_fusion.2), kind=kLoop, calls=%fused_computation.31 | loop fusion | flops 2095104 | bytes 2109440 | tf_op jit(solution)/shard_map/reduce_sum | solution.py:39
  51.4 1.9 %while.35 = (s32[]{:T(128)}, f32[1024]{0:T(1024)S(1)}, f32[1024]{0:T(1024)S(1)}, f32[1024]{0:T(1024)S(1)}, f32[1024]{0:T(1024)S(1)}, /*index=5*/f32[512,1024]{1,0:T(8,128)S(1)}, s32[]{:T(128)}, s32[]{:T(128)}) while((s32[]{:T(128)}, f32[1024]{0:T(1024)S(1)}, f32[1024]{0:T(1024)S(1)}, f32[1024]{0:T(1024)S(1)}, ...), condition=%wide.region_11.12_spmd.clone, body=%wide.region_9.11_spmd.clone.sunk | while | flops 1582083 | bytes 2154591 | solution.py:56
  51.5 0.3 maximum_reduce_fusion.7
  51.8 0.3 maximum_reduce_fusion.7
  52.1 0.3 maximum_reduce_fusion.7
  52.4 0.3 maximum_reduce_fusion.7
  52.7 0.3 maximum_reduce_fusion.7
  53.0 0.3 maximum_reduce_fusion.7
  53.4 6.4 %fusion.9 = (f32[]{:T(128)}, f32[]{:T(128)}, f32[]{:T(128)}, f32[]{:T(128)}, f32[512,1024]{0,1:T(8,128)}, /*index=5*/f32[512,1024]{0,1:T(8,128)S(1)}) fusion(f32[1024,512]{1,0:T(8,128)} %get-tuple-element.187, f32[512,1024]{0,1:T(8,128)} %get-tuple-element.173, f32[1024]{0:T(1024)S(1)} %divide_add_fusion.1, f32[512,1024]{0,1:T(8,128)} %copy-done.1, ...), kind=kLoop, calls=%fused_computation.21 | loop fusion | flops 8912892 | bytes 14688272 | tf_op jit(solution)/shard_map/reduce_sum | solution.py:88
  59.8 2.6 %maximum_bitcast_fusion = (f32[1,2]{1,0:T(1,128)S(1)}, f32[1,2]{1,0:T(1,128)S(1)}) fusion(f32[1]{0:T(128)} %bitcast.4, f32[1]{0:T(128)} %bitcast.3, f32[1]{0:T(128)} %bitcast.7, f32[1]{0:T(128)} %bitcast.6), kind=kLoop, calls=%fused_computation.61 | loop fusion | flops 4 | bytes 32 | tf_op jit(solution)/shard_map/stack | solution.py:93
  62.3 8.5 %psum.28 = f32[2,2]{1,0:T(2,128)S(1)} all-reduce(f32[2,2]{1,0:T(2,128)S(1)} %pad_maximum_fusion), channel_id=1, replica_groups=mesh['pix_0'=4,'pix_1'=8,'pix_2'=2,'band'=4] {'pix_0'}, use_global_device_ids=true, to_apply=%region_16.17 | all-reduce | flops 4 | bytes 32 | tf_op jit(solution)/shard_map/psum | solution.py:29
  70.8 16.2 %psum.29 = f32[2,2]{1,0:T(2,128)S(1)} all-reduce(f32[2,2]{1,0:T(2,128)S(1)} %psum.28), channel_id=1, replica_groups=mesh['pix_0'=4,'pix_1'=8,'pix_2'=2,'band'=4] {'pix_1'}, use_global_device_ids=true, to_apply=%region_17.18 | all-reduce | flops 4 | bytes 32 | tf_op jit(solution)/shard_map/psum | solution.py:29
  87.1 11.6 %psum.30 = f32[2,2]{1,0:T(2,128)S(1)} all-reduce(f32[2,2]{1,0:T(2,128)S(1)} %psum.29), channel_id=1, replica_groups=mesh['pix_0'=4,'pix_1'=8,'pix_2'=2,'band'=4] {'pix_2'}, use_global_device_ids=true, to_apply=%region_18.19 | all-reduce | flops 4 | bytes 32 | tf_op jit(solution)/shard_map/psum | solution.py:29
  98.7 2.9 %copy.16 = f32[512,1024]{1,0:T(8,128)} copy(f32[512,1024]{0,1:T(8,128)} %get-tuple-element.182) | data formatting | bytes 4194304
  101.5 7.7 %psum.31 = f32[2,2]{1,0:T(2,128)S(1)} all-reduce(f32[2,2]{1,0:T(2,128)S(1)} %psum.30), channel_id=1, replica_groups=mesh['pix_0'=4,'pix_1'=8,'pix_2'=2,'band'=4] {'band'}, use_global_device_ids=true, to_apply=%region_19.20 | all-reduce | flops 4 | bytes 32 | tf_op jit(solution)/shard_map/psum | solution.py:29
  109.2 0.6 multiply_sqrt_fusion
  109.8 1.8 %copy.17 = f32[512,1024]{1,0:T(8,128)} copy(f32[512,1024]{0,1:T(8,128)S(1)} %get-tuple-element.183) | data formatting | bytes 4194304
  (37 shorter events, 0.3 us)
Async XLA Ops:
  0.6 26.5 %copy-start = (f32[512,512]{1,0:T(8,128)S(1)}, f32[512,512]{1,0:T(8,128)}, u32[]{:S(2)}) copy-start(f32[512,512]{1,0:T(8,128)} %param.11) | copy-start | bytes 3145732
  2.0 0.8 copy-start.4
  3.5 21.1 %collective-permute-start = (bf16[56,1024]{1,0:T(8,128)(2,1)}, bf16[56,1024]{1,0:T(8,128)(2,1)S(1)}, u32[]{:S(2)}, u32[]{:S(2)}) collective-permute-start(bf16[56,1024]{1,0:T(8,128)(2,1)} %get-tuple-element.186), channel_id=1, source_target_pairs={{0,3},{1,0},{2,1},{3,2},{4,7},{5,4},{6,5},{7,6},{8,11},{9,8},{10,9... | collective-permute-start | bytes 344072 | tf_op jit(solution)/shard_map/ppermute | solution.py:22
  7.1 17.6 %collective-permute-start.2 = (bf16[56,1024]{1,0:T(8,128)(2,1)}, bf16[56,1024]{1,0:T(8,128)(2,1)S(1)}, u32[]{:S(2)}, u32[]{:S(2)}) collective-permute-start(bf16[56,1024]{1,0:T(8,128)(2,1)} %get-tuple-element.184), channel_id=1, source_target_pairs={{0,1},{1,2},{2,3},{3,0},{4,5},{5,6},{6,7},{7,4},{8,9},{9,10},{10,1... | collective-permute-start | bytes 344072 | tf_op jit(solution)/shard_map/ppermute | solution.py:22
  7.1 17.5 %collective-permute-start.1 = (bf16[56,1024]{1,0:T(8,128)(2,1)}, bf16[56,1024]{1,0:T(8,128)(2,1)S(1)}, u32[]{:S(2)}, u32[]{:S(2)}) collective-permute-start(bf16[56,1024]{1,0:T(8,128)(2,1)} %get-tuple-element.185), channel_id=1, source_target_pairs={{0,2},{1,3},{2,0},{3,1},{4,6},{5,7},{6,4},{7,5},{8,10},{9,11},{10,... | collective-permute-start | bytes 344072 | tf_op jit(solution)/shard_map/ppermute | solution.py:22
  10.6 16.5 %copy-start.1 = (f32[512,1024]{0,1:T(8,128)}, f32[512,1024]{0,1:T(8,128)S(1)}, u32[]{:S(2)}) copy-start(f32[512,1024]{0,1:T(8,128)S(1)} %copy.8) | copy-start | bytes 6291460
  10.7 3.7 %copy-start.5 = (bf16[56,512]{1,0:T(8,128)(2,1)S(1)}, bf16[56,512]{1,0:T(8,128)(2,1)}, u32[]{:S(2)}) copy-start(bf16[56,512]{1,0:T(8,128)(2,1)} %param.10) | copy-start | bytes 172036
  24.6 2.5 %copy-start.3 = (f32[512,1024]{0,1:T(8,128)S(1)}, f32[512,1024]{0,1:T(8,128)}, u32[]{:S(2)}) copy-start(f32[512,1024]{0,1:T(8,128)} %copy.9) | copy-start | bytes 6291460
  27.2 5.3 %copy-start.2 = (f32[1024,512]{1,0:T(8,128)}, f32[1024,512]{1,0:T(8,128)S(1)}, u32[]{:S(2)}) copy-start(f32[1024,512]{1,0:T(8,128)S(1)} %fusion.25) | copy-start | bytes 6291460
